TPU v7x, 512 devices: a whole 4x8x8 slice. The times are simulated.
512 devices in a mesh: band: 4 (over x), tile: 16 (over y_lo, z), slab: 8 (over y_hi, core).
Axes of the slice: x: 4, y: 8 (y_hi: 4, y_lo: 2; y = y_hi * 2 + y_lo), z: 8, core: 2. Of those that a mesh axis runs over, the one named last changes fastest.
Arguments:
- strength: float32 [32], P('band'), may hold values from 0.0005 to 0.5
- opacity: float32 [64, 256, 256], P('slab', 'tile'), may hold values from 0.5 to 2
- planck: float32 [64, 256, 256], P('slab', 'tile'), may hold values from 0.5 to 2
- old_populations: float32 [5, 64, 256, 256], P(None, 'slab', 'tile'), may hold values from 0.1 to 1
- line_index: int32 [32], P('band'), may hold values from 0 to 4
- line_weight: float32 [32], P('band'), may hold values from 0.2 to 1
Outputs:
- new_populations: float32 [5, 64, 256, 256], P(None, 'slab', 'tile', 'band')
- new_source: float32 [32, 64, 256, 256], P('band', 'slab', 'tile')
Inputs may be any that keep to these rules, and one draw needn't show every extreme that they name: line_index names a transition of the model atom.
All inputs are finite; a program needn't handle non-finite values.
Results may differ from a plain program's by a relative error of at most 0.0001.
Values sent between devices are 32-bit elements; how exact they have to be, the bound alone decides.
No kernel may reach another device: no remote copies, remote signals or barrier semaphores. Data moves between devices by JAX's collectives and lax.ppermute only.
A program may use at most 64 MiB of HBM per device.

v0:
```python
import jax
import jax.numpy as jnp
from jax import lax
from jax.sharding import PartitionSpec as P

LINES = 5
EPS_THERMAL = 0.1
COLLISION = 0.5
PATH_FACTOR = 1.25
TILT_SHARE = 0.4
LOWER_LEVEL = (0, 0, 1, 1, 2)
UPPER_LEVEL = (3, 4, 3, 4, 4)


def extended_2(cells, sides, width):
    for axis, dim in sides:
        count = lax.axis_size(axis)
        ends = count - 1
        head = lax.slice_in_dim(cells, 0, width, axis=dim)
        tail = lax.slice_in_dim(cells, cells.shape[dim] - width, cells.shape[dim], axis=dim)
        cells = jnp.concatenate(
            [
                lax.ppermute(tail, axis, [(i, (i + 1) % count) for i in range(ends)]),
                cells,
                lax.ppermute(head, axis, [((i + 1) % count, i) for i in range(ends)]),
            ],
            axis=dim,
        )
    return cells


def shifted(block, axis, distance):
    devices = range(lax.axis_size(axis))
    route = [(i - distance, i) for i in devices if i - distance in devices]
    return lax.ppermute(block, axis, route)


def relax(jbar, planck):
    ratios = (jbar + COLLISION * planck[None]) / (1.0 + jbar + COLLISION)
    ground = jnp.ones_like(planck)
    level_three = ratios[0]
    level_four = ratios[1]
    level_one = 0.5 * (level_three / ratios[2] + level_four / ratios[3])
    level_two = level_four / ratios[4]
    stacked = jnp.stack([ground, level_one, level_two, level_three, level_four], axis=0)
    return stacked / jnp.sum(stacked, axis=0)


def line_sources(levels_now):
    return jnp.stack(
        [
            levels_now[UPPER_LEVEL[t]] / (levels_now[LOWER_LEVEL[t]] + levels_now[UPPER_LEVEL[t]])
            for t in range(5)
        ],
        axis=0,
    )


def sweep(face_ext, strength, opacity_ext, source_ext, margin):
    intensity = face_ext
    layer_sums = []
    for plane in range(opacity_ext.shape[0]):
        attenuation = jnp.exp(-PATH_FACTOR * strength[:, None, None] * opacity_ext[plane][None])[
            :, None
        ]
        zero_column = jnp.zeros_like(intensity[:, 0, :1])
        from_left = jnp.concatenate([zero_column, intensity[:, 0, :-1]], axis=1)
        from_right = jnp.concatenate([intensity[:, 1, 1:], zero_column], axis=1)
        upwind = jnp.stack([from_left, from_right], axis=1)
        intensity = (
            attenuation * ((1.0 - TILT_SHARE) * intensity + TILT_SHARE * upwind)
            + (1.0 - attenuation) * source_ext[:, plane][:, None]
        )
        layer_sums.append(jnp.sum(intensity[:, :, margin:-margin], axis=1))
    return (intensity[:, :, margin:-margin], jnp.stack(layer_sums, axis=1))


def per_device(strength, opacity, planck, old_populations, line_index, line_weight):
    highest = lax.Precision.HIGHEST
    slab_depth, tile_rows, cells_y = opacity.shape
    freq_count = strength.shape[0]
    total_freqs = freq_count * lax.axis_size("band")
    onehot = (line_index[:, None] == jnp.arange(LINES, dtype=jnp.int32)[None, :]).astype(
        jnp.float32
    )
    weighted = onehot * line_weight[:, None] * (LINES / (2.0 * total_freqs))
    fields = jnp.concatenate([opacity[None], planck[None], old_populations], axis=0)
    fields_ext = extended_2(fields, (("tile", 2),), slab_depth)
    opacity_ext = fields_ext[0]
    planck_ext = fields_ext[1]
    levels_ext = fields_ext[2:]
    extended = tile_rows + 2 * slab_depth
    global_x = (
        lax.axis_index("tile") * tile_rows - slab_depth + jnp.arange(extended, dtype=jnp.int32)
    )
    inside = ((global_x >= 0) & (global_x < tile_rows * lax.axis_size("tile")))[None, :, None]
    lower_ext = jnp.stack([levels_ext[LOWER_LEVEL[t]] for t in range(5)], axis=0)
    upper_ext = jnp.stack([levels_ext[UPPER_LEVEL[t]] for t in range(5)], axis=0)
    denominator = jnp.where(inside, lower_ext + upper_ext, 1.0)
    line_ext = jnp.where(inside, upper_ext / denominator, 0.0)
    source_ext = jnp.where(
        inside,
        EPS_THERMAL * planck_ext[None]
        + (1.0 - EPS_THERMAL) * jnp.einsum("ft,tzxy->fzxy", onehot, line_ext, precision=highest),
        0.0,
    )
    slab_count = lax.axis_size("slab")

    def whole_step(step, carry):
        face_in, previous = carry
        face_ext = extended_2(face_in, (("tile", 2),), slab_depth)
        bottom, layer_sums = sweep(face_ext, strength, opacity_ext, source_ext, slab_depth)
        return (shifted(bottom, "slab", 1), layer_sums)

    face_start = jnp.zeros((freq_count, 2, tile_rows, cells_y), jnp.float32)
    initial = (face_start, jnp.zeros((freq_count, slab_depth, tile_rows, cells_y), jnp.float32))
    _, layer_sums = lax.fori_loop(0, slab_count, whole_step, initial)
    jbar = jnp.einsum("ft,fzxy->tzxy", weighted, layer_sums, precision=highest)
    share = cells_y // lax.axis_size("band")
    offset = lax.axis_index("band") * share
    jbar_share = lax.psum_scatter(jbar, "band", scatter_dimension=3, tiled=True)
    planck_share = lax.dynamic_slice_in_dim(planck, offset, share, 2)
    populations_share = relax(jbar_share, planck_share)
    populations_all = lax.all_gather(populations_share, "band", axis=3, tiled=True)
    new_source = EPS_THERMAL * planck[None] + (1.0 - EPS_THERMAL) * jnp.einsum(
        "ft,tzxy->fzxy", onehot, line_sources(populations_all), precision=highest
    )
    return (populations_share, new_source)


def solution(mesh):
    in_specs = (
        P("band"),
        P("slab", "tile", None),
        P("slab", "tile", None),
        P(None, "slab", "tile", None),
        P("band"),
        P("band"),
    )
    out_specs = (P(None, "slab", "tile", "band"), P("band", "slab", "tile", None))
    return jax.shard_map(
        per_device, mesh=mesh, in_specs=in_specs, out_specs=out_specs, check_vma=False
    )
```

profile of v0, /device:TPU:8, one launch (start us, length us, event | category | flops | bytes accessed | tf_op | source)
XLA Modules:
  0.0 435.0 jit_solution(6454355539191148617)
XLA Ops:
  8.7 4.3 collective-permute-start.3
  13.0 8.5 %collective-permute-start.4 = (f32[7,8,8,256]{3,2,1,0:T(8,128)S(1)}, f32[7,8,8,256]{3,2,1,0:T(8,128)}, u32[]{:S(2)}, u32[]{:S(2)}) collective-permute-start(f32[7,8,8,256]{3,2,1,0:T(8,128)S(1)} %get-tuple-element.113), channel_id=1, source_target_pairs={{8,0},{16,8},{24,16},{32,24},{40,32},{48,40},{56,48},{64,56},{72,6... | collective-permute-start | bytes 1376264 | tf_op jit(solution)/shard_map/ppermute | solution.py:25
  21.5 8.5 %collective-permute-done.3 = f32[7,8,8,256]{3,2,1,0:T(8,128)S(1)} collective-permute-done((f32[7,8,8,256]{3,2,1,0:T(8,128)S(1)}, f32[7,8,8,256]{3,2,1,0:T(8,128)S(1)}, u32[]{:S(2)}, u32[]{:S(2)}) %collective-permute-start.3) | collective-permute-done | bytes 458784 | tf_op jit(solution)/shard_map/ppermute | solution.py:23
  31.2 1.3 pad_maximum_fusion.1
  33.5 1.8 fusion.27
  35.3 2.2 fusion.26
  37.6 251.7 %while.12 = (s32[]{:T(128)}, f32[8,2,16,256]{3,2,0,1:T(8,128)S(1)}, f32[8,8,16,256]{3,2,0,1:T(8,128)}, f32[8]{0:T(128)S(1)}, f32[8,32,256]{2,1,0:T(8,128)S(1)}, /*index=5*/f32[8,8,32,256]{3,2,0,1:T(8,128)}, s32[]{:T(128)}) while((s32[]{:T(128)}, f32[8,2,16,256]{3,2,0,1:T(8,128)S(1)}, f32[8,8,16,256]{3,2,0,1:T(8,128)}, f32[8]{0:T(128)S(1)}, ...), condition=%wide.region_9.10_spmd, body=%wide.region_0.9_spmd.sunk | while | flops 24772616 | bytes 81658408 | solution.py:117
  38.6 1.9 collective-permute-start
  40.5 6.6 %collective-permute-start.1 = (f32[8,2,8,256]{3,2,0,1:T(8,128)}, f32[8,2,8,256]{3,2,0,1:T(8,128)}, u32[]{:S(2)}, u32[]{:S(2)}) collective-permute-start(f32[8,2,8,256]{3,2,0,1:T(8,128)} %get-tuple-element.218), channel_id=1, source_target_pairs={{8,0},{16,8},{24,16},{32,24},{40,32},{48,40},{56,48},{64,56},{72,6... | collective-permute-start | bytes 393224 | tf_op jit(solution)/shard_map/while/body/eval_jaxpr/ppermute | solution.py:25
  47.2 2.8 multiply_bitcast_fusion.9
  65.1 1.9 collective-permute-start
  67.0 6.0 %collective-permute-start.1 = (f32[8,2,8,256]{3,2,0,1:T(8,128)}, f32[8,2,8,256]{3,2,0,1:T(8,128)}, u32[]{:S(2)}, u32[]{:S(2)}) collective-permute-start(f32[8,2,8,256]{3,2,0,1:T(8,128)} %get-tuple-element.218), channel_id=1, source_target_pairs={{8,0},{16,8},{24,16},{32,24},{40,32},{48,40},{56,48},{64,56},{72,6... | collective-permute-start | bytes 393224 | tf_op jit(solution)/shard_map/while/body/eval_jaxpr/ppermute | solution.py:25
  73.1 2.8 multiply_bitcast_fusion.9
  87.8 6.8 %collective-permute-start.2 = (f32[8,2,16,256]{3,2,0,1:T(8,128)S(1)}, f32[8,2,16,256]{3,2,0,1:T(8,128)S(1)}, u32[]{:S(2)}, u32[]{:S(2)}) collective-permute-start(f32[8,2,16,256]{3,2,0,1:T(8,128)S(1)} %get-tuple-element.252), channel_id=1, source_target_pairs={{0,1},{1,2},{2,3},{3,4},{4,5},{5,6},{6,7},{8,9},{9,10},{10,11},{11... | collective-permute-start | bytes 786440 | tf_op jit(solution)/shard_map/while/body/eval_jaxpr/ppermute | solution.py:35
  96.6 1.9 collective-permute-start
  98.5 6.0 %collective-permute-start.1 = (f32[8,2,8,256]{3,2,0,1:T(8,128)}, f32[8,2,8,256]{3,2,0,1:T(8,128)}, u32[]{:S(2)}, u32[]{:S(2)}) collective-permute-start(f32[8,2,8,256]{3,2,0,1:T(8,128)} %get-tuple-element.218), channel_id=1, source_target_pairs={{8,0},{16,8},{24,16},{32,24},{40,32},{48,40},{56,48},{64,56},{72,6... | collective-permute-start | bytes 393224 | tf_op jit(solution)/shard_map/while/body/eval_jaxpr/ppermute | solution.py:25
  104.6 2.8 multiply_bitcast_fusion.9
  119.3 7.5 %collective-permute-start.2 = (f32[8,2,16,256]{3,2,0,1:T(8,128)S(1)}, f32[8,2,16,256]{3,2,0,1:T(8,128)S(1)}, u32[]{:S(2)}, u32[]{:S(2)}) collective-permute-start(f32[8,2,16,256]{3,2,0,1:T(8,128)S(1)} %get-tuple-element.252), channel_id=1, source_target_pairs={{0,1},{1,2},{2,3},{3,4},{4,5},{5,6},{6,7},{8,9},{9,10},{10,11},{11... | collective-permute-start | bytes 786440 | tf_op jit(solution)/shard_map/while/body/eval_jaxpr/ppermute | solution.py:35
  128.7 1.9 collective-permute-start
  130.7 6.0 %collective-permute-start.1 = (f32[8,2,8,256]{3,2,0,1:T(8,128)}, f32[8,2,8,256]{3,2,0,1:T(8,128)}, u32[]{:S(2)}, u32[]{:S(2)}) collective-permute-start(f32[8,2,8,256]{3,2,0,1:T(8,128)} %get-tuple-element.218), channel_id=1, source_target_pairs={{8,0},{16,8},{24,16},{32,24},{40,32},{48,40},{56,48},{64,56},{72,6... | collective-permute-start | bytes 393224 | tf_op jit(solution)/shard_map/while/body/eval_jaxpr/ppermute | solution.py:25
  136.8 2.8 multiply_bitcast_fusion.9
  151.5 7.6 %collective-permute-start.2 = (f32[8,2,16,256]{3,2,0,1:T(8,128)S(1)}, f32[8,2,16,256]{3,2,0,1:T(8,128)S(1)}, u32[]{:S(2)}, u32[]{:S(2)}) collective-permute-start(f32[8,2,16,256]{3,2,0,1:T(8,128)S(1)} %get-tuple-element.252), channel_id=1, source_target_pairs={{0,1},{1,2},{2,3},{3,4},{4,5},{5,6},{6,7},{8,9},{9,10},{10,11},{11... | collective-permute-start | bytes 786440 | tf_op jit(solution)/shard_map/while/body/eval_jaxpr/ppermute | solution.py:35
  160.9 1.9 collective-permute-start
  162.9 6.0 %collective-permute-start.1 = (f32[8,2,8,256]{3,2,0,1:T(8,128)}, f32[8,2,8,256]{3,2,0,1:T(8,128)}, u32[]{:S(2)}, u32[]{:S(2)}) collective-permute-start(f32[8,2,8,256]{3,2,0,1:T(8,128)} %get-tuple-element.218), channel_id=1, source_target_pairs={{8,0},{16,8},{24,16},{32,24},{40,32},{48,40},{56,48},{64,56},{72,6... | collective-permute-start | bytes 393224 | tf_op jit(solution)/shard_map/while/body/eval_jaxpr/ppermute | solution.py:25
  169.0 2.8 multiply_bitcast_fusion.9
  183.7 7.6 %collective-permute-start.2 = (f32[8,2,16,256]{3,2,0,1:T(8,128)S(1)}, f32[8,2,16,256]{3,2,0,1:T(8,128)S(1)}, u32[]{:S(2)}, u32[]{:S(2)}) collective-permute-start(f32[8,2,16,256]{3,2,0,1:T(8,128)S(1)} %get-tuple-element.252), channel_id=1, source_target_pairs={{0,1},{1,2},{2,3},{3,4},{4,5},{5,6},{6,7},{8,9},{9,10},{10,11},{11... | collective-permute-start | bytes 786440 | tf_op jit(solution)/shard_map/while/body/eval_jaxpr/ppermute | solution.py:35
  193.2 1.9 collective-permute-start
  195.1 6.0 %collective-permute-start.1 = (f32[8,2,8,256]{3,2,0,1:T(8,128)}, f32[8,2,8,256]{3,2,0,1:T(8,128)}, u32[]{:S(2)}, u32[]{:S(2)}) collective-permute-start(f32[8,2,8,256]{3,2,0,1:T(8,128)} %get-tuple-element.218), channel_id=1, source_target_pairs={{8,0},{16,8},{24,16},{32,24},{40,32},{48,40},{56,48},{64,56},{72,6... | collective-permute-start | bytes 393224 | tf_op jit(solution)/shard_map/while/body/eval_jaxpr/ppermute | solution.py:25
  201.2 2.8 multiply_bitcast_fusion.9
  215.9 7.6 %collective-permute-start.2 = (f32[8,2,16,256]{3,2,0,1:T(8,128)S(1)}, f32[8,2,16,256]{3,2,0,1:T(8,128)S(1)}, u32[]{:S(2)}, u32[]{:S(2)}) collective-permute-start(f32[8,2,16,256]{3,2,0,1:T(8,128)S(1)} %get-tuple-element.252), channel_id=1, source_target_pairs={{0,1},{1,2},{2,3},{3,4},{4,5},{5,6},{6,7},{8,9},{9,10},{10,11},{11... | collective-permute-start | bytes 786440 | tf_op jit(solution)/shard_map/while/body/eval_jaxpr/ppermute | solution.py:35
  225.4 1.9 collective-permute-start
  227.3 6.0 %collective-permute-start.1 = (f32[8,2,8,256]{3,2,0,1:T(8,128)}, f32[8,2,8,256]{3,2,0,1:T(8,128)}, u32[]{:S(2)}, u32[]{:S(2)}) collective-permute-start(f32[8,2,8,256]{3,2,0,1:T(8,128)} %get-tuple-element.218), channel_id=1, source_target_pairs={{8,0},{16,8},{24,16},{32,24},{40,32},{48,40},{56,48},{64,56},{72,6... | collective-permute-start | bytes 393224 | tf_op jit(solution)/shard_map/while/body/eval_jaxpr/ppermute | solution.py:25
  233.4 2.8 multiply_bitcast_fusion.9
  248.1 7.6 %collective-permute-start.2 = (f32[8,2,16,256]{3,2,0,1:T(8,128)S(1)}, f32[8,2,16,256]{3,2,0,1:T(8,128)S(1)}, u32[]{:S(2)}, u32[]{:S(2)}) collective-permute-start(f32[8,2,16,256]{3,2,0,1:T(8,128)S(1)} %get-tuple-element.252), channel_id=1, source_target_pairs={{0,1},{1,2},{2,3},{3,4},{4,5},{5,6},{6,7},{8,9},{9,10},{10,11},{11... | collective-permute-start | bytes 786440 | tf_op jit(solution)/shard_map/while/body/eval_jaxpr/ppermute | solution.py:35
  257.6 1.9 collective-permute-start
  259.5 6.0 %collective-permute-start.1 = (f32[8,2,8,256]{3,2,0,1:T(8,128)}, f32[8,2,8,256]{3,2,0,1:T(8,128)}, u32[]{:S(2)}, u32[]{:S(2)}) collective-permute-start(f32[8,2,8,256]{3,2,0,1:T(8,128)} %get-tuple-element.218), channel_id=1, source_target_pairs={{8,0},{16,8},{24,16},{32,24},{40,32},{48,40},{56,48},{64,56},{72,6... | collective-permute-start | bytes 393224 | tf_op jit(solution)/shard_map/while/body/eval_jaxpr/ppermute | solution.py:25
  265.6 2.8 multiply_bitcast_fusion.9
  280.3 7.8 %collective-permute-start.2 = (f32[8,2,16,256]{3,2,0,1:T(8,128)S(1)}, f32[8,2,16,256]{3,2,0,1:T(8,128)S(1)}, u32[]{:S(2)}, u32[]{:S(2)}) collective-permute-start(f32[8,2,16,256]{3,2,0,1:T(8,128)S(1)} %get-tuple-element.252), channel_id=1, source_target_pairs={{0,1},{1,2},{2,3},{3,4},{4,5},{5,6},{6,7},{8,9},{9,10},{10,11},{11... | collective-permute-start | bytes 786440 | tf_op jit(solution)/shard_map/while/body/eval_jaxpr/ppermute | solution.py:35
  289.3 2.8 fusion.33
  292.1 13.8 %copy.27 = f32[5,8,16,256]{0,2,1,3:T(8,128)} copy(f32[5,8,16,256]{3,0,2,1:T(8,128)S(1)} %fusion.33) | data formatting | bytes 1310720
  305.9 11.9 %reshape.106 = f32[256,640]{1,0:T(8,128)} reshape(f32[256,8,16,5]{3,2,1,0:T(8,128)} %bitcast.211) | data formatting | bytes 1310720
  318.6 43.0 %reduce-scatter.4.cloned.1.call-done = f32[64,640]{1,0:T(8,128)} async-done(((f32[256,640]{1,0:T(8,128)}), f32[64,640]{1,0:T(8,128)}) %reduce-scatter.4.cloned.1.call-update) | async-done | bytes 163856
  361.5 6.2 %reshape.107 = f32[64,8,16,5]{3,2,1,0:T(8,128)} reshape(f32[64,640]{1,0:T(8,128)} %reduce-scatter.4.cloned.1.call-done) | data formatting | bytes 327680
  367.8 3.8 copy.28
  373.9 45.2 %all_gather.3 = f32[5,8,16,256]{2,1,0,3:T(8,128)S(1)} all-gather(f32[5,8,16,64]{2,1,0,3:T(8,128)S(1)} %copy.14), channel_id=1, replica_groups=mesh['band'=4,'tile'=16,'slab'=8] {'band'}, dimensions={3}, use_global_device_ids=true | all-gather | bytes 819200 | tf_op jit(solution)/shard_map/all_gather | solution.py:124
  419.1 1.7 fusion.56
  420.7 1.5 copy.31
  422.3 1.5 copy.33
  (630 shorter events, 120.4 us)
Async XLA Ops:
  7.2 354.4 %reduce-scatter.4.cloned.1.call-start = ((), (), s32[]{:S(2)}) async-start(), calls=%async_computation.1 | async-start | bytes 819200
  7.2 24.0 %copy-start.7 = (f32[5,8,16,256]{3,2,1,0:T(8,128)S(1)}, f32[5,8,16,256]{3,2,1,0:T(8,128)}, u32[]{:S(2)}) copy-start(f32[5,8,16,256]{3,2,1,0:T(8,128)} %param.11) | copy-start | bytes 1966084
  7.2 24.0 %copy-start.8 = (f32[8,16,256]{2,1,0:T(8,128)S(1)}, f32[8,16,256]{2,1,0:T(8,128)}, u32[]{:S(2)}) copy-start(f32[8,16,256]{2,1,0:T(8,128)} %param.10) | copy-start | bytes 393220
  7.2 24.0 %copy-start.11 = (f32[8,16,256]{2,1,0:T(8,128)S(1)}, f32[8,16,256]{2,1,0:T(8,128)}, u32[]{:S(2)}) copy-start(f32[8,16,256]{2,1,0:T(8,128)} %param.9) | copy-start | bytes 393220
  8.7 21.3 %collective-permute-start.3 = (f32[7,8,8,256]{3,2,1,0:T(8,128)S(1)}, f32[7,8,8,256]{3,2,1,0:T(8,128)S(1)}, u32[]{:S(2)}, u32[]{:S(2)}) collective-permute-start(f32[7,8,8,256]{3,2,1,0:T(8,128)S(1)} %get-tuple-element.112), channel_id=1, source_target_pairs={{0,8},{8,16},{16,24},{24,32},{32,40},{40,48},{48,56},{56,64},{64,7... | collective-permute-start | bytes 1376264 | tf_op jit(solution)/shard_map/ppermute | solution.py:23
  13.0 18.2 %collective-permute-start.4 = (f32[7,8,8,256]{3,2,1,0:T(8,128)S(1)}, f32[7,8,8,256]{3,2,1,0:T(8,128)}, u32[]{:S(2)}, u32[]{:S(2)}) collective-permute-start(f32[7,8,8,256]{3,2,1,0:T(8,128)S(1)} %get-tuple-element.113), channel_id=1, source_target_pairs={{8,0},{16,8},{24,16},{32,24},{40,32},{48,40},{56,48},{64,56},{72,6... | collective-permute-start | bytes 1376264 | tf_op jit(solution)/shard_map/ppermute | solution.py:25
  37.5 251.7 %copy-start.15 = (f32[8]{0:T(128)S(1)}, f32[8]{0:T(128)}, u32[]{:S(2)}) copy-start(f32[8]{0:T(128)} %param.13) | copy-start | bytes 100
  37.7 9.4 %copy-start.1 = (f32[8,2,16,256]{3,2,0,1:T(8,128)}, f32[8,2,16,256]{3,2,0,1:T(8,128)S(1)}, u32[]{:S(2)}) copy-start(f32[8,2,16,256]{3,2,0,1:T(8,128)S(1)} %get-tuple-element.263) | copy-start | bytes 786436 | tf_op jit(solution)/shard_map/while
  37.8 9.4 %copy-start.5 = (f32[8,32,256]{2,1,0:T(8,128)}, f32[8,32,256]{2,1,0:T(8,128)S(1)}, u32[]{:S(2)}) copy-start(f32[8,32,256]{2,1,0:T(8,128)S(1)} %get-tuple-element.273) | copy-start | bytes 786436 | tf_op jit(solution)/shard_map/while
  38.6 13.2 %collective-permute-start = (f32[8,2,8,256]{3,2,0,1:T(8,128)}, f32[8,2,8,256]{3,2,0,1:T(8,128)}, u32[]{:S(2)}, u32[]{:S(2)}) collective-permute-start(f32[8,2,8,256]{3,2,0,1:T(8,128)} %get-tuple-element.217), channel_id=1, source_target_pairs={{0,8},{8,16},{16,24},{24,32},{32,40},{40,48},{48,56},{56,64},{64,7... | collective-permute-start | bytes 393224 | tf_op jit(solution)/shard_map/while/body/eval_jaxpr/ppermute | solution.py:23
  40.5 13.1 %collective-permute-start.1 = (f32[8,2,8,256]{3,2,0,1:T(8,128)}, f32[8,2,8,256]{3,2,0,1:T(8,128)}, u32[]{:S(2)}, u32[]{:S(2)}) collective-permute-start(f32[8,2,8,256]{3,2,0,1:T(8,128)} %get-tuple-element.218), channel_id=1, source_target_pairs={{8,0},{16,8},{24,16},{32,24},{40,32},{48,40},{56,48},{64,56},{72,6... | collective-permute-start | bytes 393224 | tf_op jit(solution)/shard_map/while/body/eval_jaxpr/ppermute | solution.py:25
  61.9 2.4 collective-permute-start.2
  64.3 8.8 %copy-start.1 = (f32[8,2,16,256]{3,2,0,1:T(8,128)}, f32[8,2,16,256]{3,2,0,1:T(8,128)S(1)}, u32[]{:S(2)}) copy-start(f32[8,2,16,256]{3,2,0,1:T(8,128)S(1)} %get-tuple-element.263) | copy-start | bytes 786436 | tf_op jit(solution)/shard_map/while
  64.3 8.8 %copy-start.5 = (f32[8,32,256]{2,1,0:T(8,128)}, f32[8,32,256]{2,1,0:T(8,128)S(1)}, u32[]{:S(2)}) copy-start(f32[8,32,256]{2,1,0:T(8,128)S(1)} %get-tuple-element.273) | copy-start | bytes 786436 | tf_op jit(solution)/shard_map/while
  65.1 12.6 %collective-permute-start = (f32[8,2,8,256]{3,2,0,1:T(8,128)}, f32[8,2,8,256]{3,2,0,1:T(8,128)}, u32[]{:S(2)}, u32[]{:S(2)}) collective-permute-start(f32[8,2,8,256]{3,2,0,1:T(8,128)} %get-tuple-element.217), channel_id=1, source_target_pairs={{0,8},{8,16},{16,24},{24,32},{32,40},{40,48},{48,56},{56,64},{64,7... | collective-permute-start | bytes 393224 | tf_op jit(solution)/shard_map/while/body/eval_jaxpr/ppermute | solution.py:23
  67.0 12.6 %collective-permute-start.1 = (f32[8,2,8,256]{3,2,0,1:T(8,128)}, f32[8,2,8,256]{3,2,0,1:T(8,128)}, u32[]{:S(2)}, u32[]{:S(2)}) collective-permute-start(f32[8,2,8,256]{3,2,0,1:T(8,128)} %get-tuple-element.218), channel_id=1, source_target_pairs={{8,0},{16,8},{24,16},{32,24},{40,32},{48,40},{56,48},{64,56},{72,6... | collective-permute-start | bytes 393224 | tf_op jit(solution)/shard_map/while/body/eval_jaxpr/ppermute | solution.py:25
  87.8 8.0 %collective-permute-start.2 = (f32[8,2,16,256]{3,2,0,1:T(8,128)S(1)}, f32[8,2,16,256]{3,2,0,1:T(8,128)S(1)}, u32[]{:S(2)}, u32[]{:S(2)}) collective-permute-start(f32[8,2,16,256]{3,2,0,1:T(8,128)S(1)} %get-tuple-element.252), channel_id=1, source_target_pairs={{0,1},{1,2},{2,3},{3,4},{4,5},{5,6},{6,7},{8,9},{9,10},{10,11},{11... | collective-permute-start | bytes 786440 | tf_op jit(solution)/shard_map/while/body/eval_jaxpr/ppermute | solution.py:35
  95.8 8.8 %copy-start.1 = (f32[8,2,16,256]{3,2,0,1:T(8,128)}, f32[8,2,16,256]{3,2,0,1:T(8,128)S(1)}, u32[]{:S(2)}) copy-start(f32[8,2,16,256]{3,2,0,1:T(8,128)S(1)} %get-tuple-element.263) | copy-start | bytes 786436 | tf_op jit(solution)/shard_map/while
  95.8 8.8 %copy-start.5 = (f32[8,32,256]{2,1,0:T(8,128)}, f32[8,32,256]{2,1,0:T(8,128)S(1)}, u32[]{:S(2)}) copy-start(f32[8,32,256]{2,1,0:T(8,128)S(1)} %get-tuple-element.273) | copy-start | bytes 786436 | tf_op jit(solution)/shard_map/while
  96.6 12.6 %collective-permute-start = (f32[8,2,8,256]{3,2,0,1:T(8,128)}, f32[8,2,8,256]{3,2,0,1:T(8,128)}, u32[]{:S(2)}, u32[]{:S(2)}) collective-permute-start(f32[8,2,8,256]{3,2,0,1:T(8,128)} %get-tuple-element.217), channel_id=1, source_target_pairs={{0,8},{8,16},{16,24},{24,32},{32,40},{40,48},{48,56},{56,64},{64,7... | collective-permute-start | bytes 393224 | tf_op jit(solution)/shard_map/while/body/eval_jaxpr/ppermute | solution.py:23
  98.5 12.6 %collective-permute-start.1 = (f32[8,2,8,256]{3,2,0,1:T(8,128)}, f32[8,2,8,256]{3,2,0,1:T(8,128)}, u32[]{:S(2)}, u32[]{:S(2)}) collective-permute-start(f32[8,2,8,256]{3,2,0,1:T(8,128)} %get-tuple-element.218), channel_id=1, source_target_pairs={{8,0},{16,8},{24,16},{32,24},{40,32},{48,40},{56,48},{64,56},{72,6... | collective-permute-start | bytes 393224 | tf_op jit(solution)/shard_map/while/body/eval_jaxpr/ppermute | solution.py:25
  119.3 8.6 %collective-permute-start.2 = (f32[8,2,16,256]{3,2,0,1:T(8,128)S(1)}, f32[8,2,16,256]{3,2,0,1:T(8,128)S(1)}, u32[]{:S(2)}, u32[]{:S(2)}) collective-permute-start(f32[8,2,16,256]{3,2,0,1:T(8,128)S(1)} %get-tuple-element.252), channel_id=1, source_target_pairs={{0,1},{1,2},{2,3},{3,4},{4,5},{5,6},{6,7},{8,9},{9,10},{10,11},{11... | collective-permute-start | bytes 786440 | tf_op jit(solution)/shard_map/while/body/eval_jaxpr/ppermute | solution.py:35
  128.0 8.8 %copy-start.1 = (f32[8,2,16,256]{3,2,0,1:T(8,128)}, f32[8,2,16,256]{3,2,0,1:T(8,128)S(1)}, u32[]{:S(2)}) copy-start(f32[8,2,16,256]{3,2,0,1:T(8,128)S(1)} %get-tuple-element.263) | copy-start | bytes 786436 | tf_op jit(solution)/shard_map/while
  128.0 8.8 %copy-start.5 = (f32[8,32,256]{2,1,0:T(8,128)}, f32[8,32,256]{2,1,0:T(8,128)S(1)}, u32[]{:S(2)}) copy-start(f32[8,32,256]{2,1,0:T(8,128)S(1)} %get-tuple-element.273) | copy-start | bytes 786436 | tf_op jit(solution)/shard_map/while
  128.7 12.6 %collective-permute-start = (f32[8,2,8,256]{3,2,0,1:T(8,128)}, f32[8,2,8,256]{3,2,0,1:T(8,128)}, u32[]{:S(2)}, u32[]{:S(2)}) collective-permute-start(f32[8,2,8,256]{3,2,0,1:T(8,128)} %get-tuple-element.217), channel_id=1, source_target_pairs={{0,8},{8,16},{16,24},{24,32},{32,40},{40,48},{48,56},{56,64},{64,7... | collective-permute-start | bytes 393224 | tf_op jit(solution)/shard_map/while/body/eval_jaxpr/ppermute | solution.py:23
  130.7 12.6 %collective-permute-start.1 = (f32[8,2,8,256]{3,2,0,1:T(8,128)}, f32[8,2,8,256]{3,2,0,1:T(8,128)}, u32[]{:S(2)}, u32[]{:S(2)}) collective-permute-start(f32[8,2,8,256]{3,2,0,1:T(8,128)} %get-tuple-element.218), channel_id=1, source_target_pairs={{8,0},{16,8},{24,16},{32,24},{40,32},{48,40},{56,48},{64,56},{72,6... | collective-permute-start | bytes 393224 | tf_op jit(solution)/shard_map/while/body/eval_jaxpr/ppermute | solution.py:25
  151.5 8.7 %collective-permute-start.2 = (f32[8,2,16,256]{3,2,0,1:T(8,128)S(1)}, f32[8,2,16,256]{3,2,0,1:T(8,128)S(1)}, u32[]{:S(2)}, u32[]{:S(2)}) collective-permute-start(f32[8,2,16,256]{3,2,0,1:T(8,128)S(1)} %get-tuple-element.252), channel_id=1, source_target_pairs={{0,1},{1,2},{2,3},{3,4},{4,5},{5,6},{6,7},{8,9},{9,10},{10,11},{11... | collective-permute-start | bytes 786440 | tf_op jit(solution)/shard_map/while/body/eval_jaxpr/ppermute | solution.py:35
  160.2 8.8 %copy-start.1 = (f32[8,2,16,256]{3,2,0,1:T(8,128)}, f32[8,2,16,256]{3,2,0,1:T(8,128)S(1)}, u32[]{:S(2)}) copy-start(f32[8,2,16,256]{3,2,0,1:T(8,128)S(1)} %get-tuple-element.263) | copy-start | bytes 786436 | tf_op jit(solution)/shard_map/while
  160.2 8.8 %copy-start.5 = (f32[8,32,256]{2,1,0:T(8,128)}, f32[8,32,256]{2,1,0:T(8,128)S(1)}, u32[]{:S(2)}) copy-start(f32[8,32,256]{2,1,0:T(8,128)S(1)} %get-tuple-element.273) | copy-start | bytes 786436 | tf_op jit(solution)/shard_map/while
  160.9 12.6 %collective-permute-start = (f32[8,2,8,256]{3,2,0,1:T(8,128)}, f32[8,2,8,256]{3,2,0,1:T(8,128)}, u32[]{:S(2)}, u32[]{:S(2)}) collective-permute-start(f32[8,2,8,256]{3,2,0,1:T(8,128)} %get-tuple-element.217), channel_id=1, source_target_pairs={{0,8},{8,16},{16,24},{24,32},{32,40},{40,48},{48,56},{56,64},{64,7... | collective-permute-start | bytes 393224 | tf_op jit(solution)/shard_map/while/body/eval_jaxpr/ppermute | solution.py:23
  162.9 12.6 %collective-permute-start.1 = (f32[8,2,8,256]{3,2,0,1:T(8,128)}, f32[8,2,8,256]{3,2,0,1:T(8,128)}, u32[]{:S(2)}, u32[]{:S(2)}) collective-permute-start(f32[8,2,8,256]{3,2,0,1:T(8,128)} %get-tuple-element.218), channel_id=1, source_target_pairs={{8,0},{16,8},{24,16},{32,24},{40,32},{48,40},{56,48},{64,56},{72,6... | collective-permute-start | bytes 393224 | tf_op jit(solution)/shard_map/while/body/eval_jaxpr/ppermute | solution.py:25
  183.7 8.7 %collective-permute-start.2 = (f32[8,2,16,256]{3,2,0,1:T(8,128)S(1)}, f32[8,2,16,256]{3,2,0,1:T(8,128)S(1)}, u32[]{:S(2)}, u32[]{:S(2)}) collective-permute-start(f32[8,2,16,256]{3,2,0,1:T(8,128)S(1)} %get-tuple-element.252), channel_id=1, source_target_pairs={{0,1},{1,2},{2,3},{3,4},{4,5},{5,6},{6,7},{8,9},{9,10},{10,11},{11... | collective-permute-start | bytes 786440 | tf_op jit(solution)/shard_map/while/body/eval_jaxpr/ppermute | solution.py:35
  192.4 8.8 %copy-start.1 = (f32[8,2,16,256]{3,2,0,1:T(8,128)}, f32[8,2,16,256]{3,2,0,1:T(8,128)S(1)}, u32[]{:S(2)}) copy-start(f32[8,2,16,256]{3,2,0,1:T(8,128)S(1)} %get-tuple-element.263) | copy-start | bytes 786436 | tf_op jit(solution)/shard_map/while
  192.4 8.8 %copy-start.5 = (f32[8,32,256]{2,1,0:T(8,128)}, f32[8,32,256]{2,1,0:T(8,128)S(1)}, u32[]{:S(2)}) copy-start(f32[8,32,256]{2,1,0:T(8,128)S(1)} %get-tuple-element.273) | copy-start | bytes 786436 | tf_op jit(solution)/shard_map/while
  193.2 12.6 %collective-permute-start = (f32[8,2,8,256]{3,2,0,1:T(8,128)}, f32[8,2,8,256]{3,2,0,1:T(8,128)}, u32[]{:S(2)}, u32[]{:S(2)}) collective-permute-start(f32[8,2,8,256]{3,2,0,1:T(8,128)} %get-tuple-element.217), channel_id=1, source_target_pairs={{0,8},{8,16},{16,24},{24,32},{32,40},{40,48},{48,56},{56,64},{64,7... | collective-permute-start | bytes 393224 | tf_op jit(solution)/shard_map/while/body/eval_jaxpr/ppermute | solution.py:23
  195.1 12.6 %collective-permute-start.1 = (f32[8,2,8,256]{3,2,0,1:T(8,128)}, f32[8,2,8,256]{3,2,0,1:T(8,128)}, u32[]{:S(2)}, u32[]{:S(2)}) collective-permute-start(f32[8,2,8,256]{3,2,0,1:T(8,128)} %get-tuple-element.218), channel_id=1, source_target_pairs={{8,0},{16,8},{24,16},{32,24},{40,32},{48,40},{56,48},{64,56},{72,6... | collective-permute-start | bytes 393224 | tf_op jit(solution)/shard_map/while/body/eval_jaxpr/ppermute | solution.py:25
  215.9 8.7 %collective-permute-start.2 = (f32[8,2,16,256]{3,2,0,1:T(8,128)S(1)}, f32[8,2,16,256]{3,2,0,1:T(8,128)S(1)}, u32[]{:S(2)}, u32[]{:S(2)}) collective-permute-start(f32[8,2,16,256]{3,2,0,1:T(8,128)S(1)} %get-tuple-element.252), channel_id=1, source_target_pairs={{0,1},{1,2},{2,3},{3,4},{4,5},{5,6},{6,7},{8,9},{9,10},{10,11},{11... | collective-permute-start | bytes 786440 | tf_op jit(solution)/shard_map/while/body/eval_jaxpr/ppermute | solution.py:35
  224.6 8.8 %copy-start.1 = (f32[8,2,16,256]{3,2,0,1:T(8,128)}, f32[8,2,16,256]{3,2,0,1:T(8,128)S(1)}, u32[]{:S(2)}) copy-start(f32[8,2,16,256]{3,2,0,1:T(8,128)S(1)} %get-tuple-element.263) | copy-start | bytes 786436 | tf_op jit(solution)/shard_map/while
  224.6 8.8 %copy-start.5 = (f32[8,32,256]{2,1,0:T(8,128)}, f32[8,32,256]{2,1,0:T(8,128)S(1)}, u32[]{:S(2)}) copy-start(f32[8,32,256]{2,1,0:T(8,128)S(1)} %get-tuple-element.273) | copy-start | bytes 786436 | tf_op jit(solution)/shard_map/while
  225.4 12.6 %collective-permute-start = (f32[8,2,8,256]{3,2,0,1:T(8,128)}, f32[8,2,8,256]{3,2,0,1:T(8,128)}, u32[]{:S(2)}, u32[]{:S(2)}) collective-permute-start(f32[8,2,8,256]{3,2,0,1:T(8,128)} %get-tuple-element.217), channel_id=1, source_target_pairs={{0,8},{8,16},{16,24},{24,32},{32,40},{40,48},{48,56},{56,64},{64,7... | collective-permute-start | bytes 393224 | tf_op jit(solution)/shard_map/while/body/eval_jaxpr/ppermute | solution.py:23
  227.3 12.6 %collective-permute-start.1 = (f32[8,2,8,256]{3,2,0,1:T(8,128)}, f32[8,2,8,256]{3,2,0,1:T(8,128)}, u32[]{:S(2)}, u32[]{:S(2)}) collective-permute-start(f32[8,2,8,256]{3,2,0,1:T(8,128)} %get-tuple-element.218), channel_id=1, source_target_pairs={{8,0},{16,8},{24,16},{32,24},{40,32},{48,40},{56,48},{64,56},{72,6... | collective-permute-start | bytes 393224 | tf_op jit(solution)/shard_map/while/body/eval_jaxpr/ppermute | solution.py:25
  248.1 8.7 %collective-permute-start.2 = (f32[8,2,16,256]{3,2,0,1:T(8,128)S(1)}, f32[8,2,16,256]{3,2,0,1:T(8,128)S(1)}, u32[]{:S(2)}, u32[]{:S(2)}) collective-permute-start(f32[8,2,16,256]{3,2,0,1:T(8,128)S(1)} %get-tuple-element.252), channel_id=1, source_target_pairs={{0,1},{1,2},{2,3},{3,4},{4,5},{5,6},{6,7},{8,9},{9,10},{10,11},{11... | collective-permute-start | bytes 786440 | tf_op jit(solution)/shard_map/while/body/eval_jaxpr/ppermute | solution.py:35
  256.8 8.8 %copy-start.5 = (f32[8,32,256]{2,1,0:T(8,128)}, f32[8,32,256]{2,1,0:T(8,128)S(1)}, u32[]{:S(2)}) copy-start(f32[8,32,256]{2,1,0:T(8,128)S(1)} %get-tuple-element.273) | copy-start | bytes 786436 | tf_op jit(solution)/shard_map/while
  257.6 12.6 %collective-permute-start = (f32[8,2,8,256]{3,2,0,1:T(8,128)}, f32[8,2,8,256]{3,2,0,1:T(8,128)}, u32[]{:S(2)}, u32[]{:S(2)}) collective-permute-start(f32[8,2,8,256]{3,2,0,1:T(8,128)} %get-tuple-element.217), channel_id=1, source_target_pairs={{0,8},{8,16},{16,24},{24,32},{32,40},{40,48},{48,56},{56,64},{64,7... | collective-permute-start | bytes 393224 | tf_op jit(solution)/shard_map/while/body/eval_jaxpr/ppermute | solution.py:23
  259.5 12.6 %collective-permute-start.1 = (f32[8,2,8,256]{3,2,0,1:T(8,128)}, f32[8,2,8,256]{3,2,0,1:T(8,128)}, u32[]{:S(2)}, u32[]{:S(2)}) collective-permute-start(f32[8,2,8,256]{3,2,0,1:T(8,128)} %get-tuple-element.218), channel_id=1, source_target_pairs={{8,0},{16,8},{24,16},{32,24},{40,32},{48,40},{56,48},{64,56},{72,6... | collective-permute-start | bytes 393224 | tf_op jit(solution)/shard_map/while/body/eval_jaxpr/ppermute | solution.py:25
  280.2 9.0 %copy-start.6 = (f32[8,32,256]{2,1,0:T(8,128)S(1)}, f32[8,32,256]{2,1,0:T(8,128)}, u32[]{:S(2)}) copy-start(f32[8,32,256]{2,1,0:T(8,128)} %copy-done.5) | copy-start | bytes 786436 | tf_op jit(solution)/shard_map/while
  280.3 9.0 %collective-permute-start.2 = (f32[8,2,16,256]{3,2,0,1:T(8,128)S(1)}, f32[8,2,16,256]{3,2,0,1:T(8,128)S(1)}, u32[]{:S(2)}, u32[]{:S(2)}) collective-permute-start(f32[8,2,16,256]{3,2,0,1:T(8,128)S(1)} %get-tuple-element.252), channel_id=1, source_target_pairs={{0,1},{1,2},{2,3},{3,4},{4,5},{5,6},{6,7},{8,9},{9,10},{10,11},{11... | collective-permute-start | bytes 786440 | tf_op jit(solution)/shard_map/while/body/eval_jaxpr/ppermute | solution.py:35
  305.9 11.9 %copy-start.9 = (f32[8,16,256]{2,1,0:T(8,128)S(1)}, f32[8,16,256]{2,1,0:T(8,128)}, u32[]{:S(2)}) copy-start(f32[8,16,256]{2,1,0:T(8,128)} %param.10) | copy-start | bytes 393220
  (52 other events, 107.1 us)
Sparse Core Ops, SparseCore 0:
  317.9 43.5 reduce-scatter.3
where the time goes:
time: 438 us; the launch traced here: 435 us
  starting transfers between devices  131 us (30%)
  local copies, waits for them, and re-layouts  107 us (24%)
  other arithmetic  69.3 us (16%)
  waiting for transfers between devices  59.8 us (14%)
  blocking collectives  45.2 us (10%)
  between operations  14.3 us (3%)
  matrix products  5.26 us (1%)
    ppermute x9, starting transfers between devices, extended_2(): lax.ppermute(head, axis, [((i + 1) % count, i) for i in range(ends)])  57.3 us
    ppermute x8, starting transfers between devices, shifted(): return lax.ppermute(block, axis, route)  53.7 us
    add x64, other arithmetic, sweep(): attenuation * ((1.0 - TILT_SHARE) * intensity + TILT_SHARE * upwind)  51.4 us
    all_gather x1, blocking collectives, per_device(): lax.all_gather(populations_share, 'band', axis=3, tiled=True)  45.2 us
    unnamed x29, local copies, waits for them, and re-layouts  43.1 us
    unnamed x2, waiting for transfers between devices  43 us
    while x200, local copies, waits for them, and re-layouts  35.4 us
    ppermute x9, starting transfers between devices, extended_2(): lax.ppermute(tail, axis, [(i, (i + 1) % count) for i in range(ends)])  19.6 us
  transfers between devices with their start and end apart: 27, of which 11 were waited for; matrix products, arithmetic and copies ran while one was open for 12% of the time, Pallas kernels for 0%

commit v1 on v0

--- a/solution.py
+++ b/solution.py
@@ -121,7 +121,10 @@
     jbar_share = lax.psum_scatter(jbar, "band", scatter_dimension=3, tiled=True)
     planck_share = lax.dynamic_slice_in_dim(planck, offset, share, 2)
     populations_share = relax(jbar_share, planck_share)
-    populations_all = lax.all_gather(populations_share, "band", axis=3, tiled=True)
+    devices_2 = lax.axis_size("band")
+    blocks = jnp.stack([populations_share for _ in range(devices_2)])
+    blocks = lax.all_to_all(blocks, "band", split_axis=0, concat_axis=0)
+    populations_all = jnp.concatenate(blocks, axis=3)
     new_source = EPS_THERMAL * planck[None] + (1.0 - EPS_THERMAL) * jnp.einsum(
         "ft,tzxy->fzxy", onehot, line_sources(populations_all), precision=highest
     )

time: 438 us -> 407 us (0.929)
  blocking collectives: 45.2 us -> 0 us
  waiting for transfers between devices: 59.8 us -> 70.4 us
    all_gather x1 -> x0, blocking collectives: 45.2 us -> none  [per_device(): lax.all_gather(populations_share, 'band', axis=3, tiled=True)]
    all_to_all x0 -> x1, waiting for transfers between devices: none -> 9.91 us  [per_device(): blocks = lax.all_to_all(blocks, 'band', split_axis=0, concat_axis=0)]
    unnamed x29 -> x26, local copies, waits for them, and re-layouts: 43.1 us -> 40.5 us
  transfers between devices with their start and end apart: 27 -> 28, of which waited for: 11 -> 12; matrix products, arithmetic and copies ran while one was open for 12% -> 13% of each run, Pallas kernels for 0% -> 0%
where the time goes in v1:
time: 407 us; the launch traced here: 404 us
  starting transfers between devices  134 us (33%)
  local copies, waits for them, and re-layouts  105 us (26%)
  other arithmetic  71.1 us (17%)
  waiting for transfers between devices  70.4 us (17%)
  between operations  14.4 us (4%)
  matrix products  5.26 us (1%)
    ppermute x9, starting transfers between devices, extended_2(): lax.ppermute(head, axis, [((i + 1) % count, i) for i in range(ends)])  57.3 us
    ppermute x8, starting transfers between devices, shifted(): return lax.ppermute(block, axis, route)  53.7 us
    add x64, other arithmetic, sweep(): attenuation * ((1.0 - TILT_SHARE) * intensity + TILT_SHARE * upwind)  51.4 us
    unnamed x2, waiting for transfers between devices  43.6 us
    unnamed x26, local copies, waits for them, and re-layouts  40.5 us
    while x200, local copies, waits for them, and re-layouts  35.4 us
    ppermute x9, starting transfers between devices, extended_2(): lax.ppermute(tail, axis, [(i, (i + 1) % count) for i in range(ends)])  19.6 us
    all_to_all x1, waiting for transfers between devices, per_device(): blocks = lax.all_to_all(blocks, 'band', split_axis=0, concat_axis=0)  9.91 us
  transfers between devices with their start and end apart: 28, of which 12 were waited for; matrix products, arithmetic and copies ran while one was open for 13% of the time, Pallas kernels for 0%

profile of v1, /device:TPU:8, one launch (start us, length us, event | category | flops | bytes accessed | tf_op | source)
XLA Modules:
  0.0 404.1 jit_solution(13068347927799107739)
XLA Ops:
  8.7 4.3 %collective-permute-start.3 = (f32[7,8,8,256]{3,2,1,0:T(8,128)S(1)}, f32[7,8,8,256]{3,2,1,0:T(8,128)S(1)}, u32[]{:S(2)}, u32[]{:S(2)}) collective-permute-start(f32[7,8,8,256]{3,2,1,0:T(8,128)S(1)} %get-tuple-element.112), channel_id=1, source_target_pairs={{0,8},{8,16},{16,24},{24,32},{32,40},{40,48},{48,56},{56,64},{64,7... | collective-permute-start | bytes 1376264 | tf_op jit(solution)/shard_map/ppermute | solution.py:23
  13.0 8.5 %collective-permute-start.4 = (f32[7,8,8,256]{3,2,1,0:T(8,128)S(1)}, f32[7,8,8,256]{3,2,1,0:T(8,128)}, u32[]{:S(2)}, u32[]{:S(2)}) collective-permute-start(f32[7,8,8,256]{3,2,1,0:T(8,128)S(1)} %get-tuple-element.113), channel_id=1, source_target_pairs={{8,0},{16,8},{24,16},{32,24},{40,32},{48,40},{56,48},{64,56},{72,6... | collective-permute-start | bytes 1376264 | tf_op jit(solution)/shard_map/ppermute | solution.py:25
  21.5 8.5 %collective-permute-done.3 = f32[7,8,8,256]{3,2,1,0:T(8,128)S(1)} collective-permute-done((f32[7,8,8,256]{3,2,1,0:T(8,128)S(1)}, f32[7,8,8,256]{3,2,1,0:T(8,128)S(1)}, u32[]{:S(2)}, u32[]{:S(2)}) %collective-permute-start.3) | collective-permute-done | bytes 458784 | tf_op jit(solution)/shard_map/ppermute | solution.py:23
  31.2 1.3 pad_maximum_fusion.1
  33.5 1.8 fusion.27
  35.3 2.2 fusion.26
  37.5 251.9 %while.12 = (s32[]{:T(128)}, f32[8,2,16,256]{3,2,0,1:T(8,128)S(1)}, f32[8,8,16,256]{3,2,0,1:T(8,128)}, f32[8]{0:T(128)S(1)}, f32[8,32,256]{2,1,0:T(8,128)S(1)}, /*index=5*/f32[8,8,32,256]{3,2,0,1:T(8,128)}, s32[]{:T(128)}) while((s32[]{:T(128)}, f32[8,2,16,256]{3,2,0,1:T(8,128)S(1)}, f32[8,8,16,256]{3,2,0,1:T(8,128)}, f32[8]{0:T(128)S(1)}, ...), condition=%wide.region_9.10_spmd, body=%wide.region_0.9_spmd.sunk | while | flops 24772616 | bytes 81658408 | solution.py:117
  38.5 1.9 collective-permute-start
  40.5 6.6 %collective-permute-start.1 = (f32[8,2,8,256]{3,2,0,1:T(8,128)}, f32[8,2,8,256]{3,2,0,1:T(8,128)}, u32[]{:S(2)}, u32[]{:S(2)}) collective-permute-start(f32[8,2,8,256]{3,2,0,1:T(8,128)} %get-tuple-element.218), channel_id=1, source_target_pairs={{8,0},{16,8},{24,16},{32,24},{40,32},{48,40},{56,48},{64,56},{72,6... | collective-permute-start | bytes 393224 | tf_op jit(solution)/shard_map/while/body/eval_jaxpr/ppermute | solution.py:25
  47.1 2.8 multiply_bitcast_fusion.9
  65.1 1.9 collective-permute-start
  67.0 6.0 %collective-permute-start.1 = (f32[8,2,8,256]{3,2,0,1:T(8,128)}, f32[8,2,8,256]{3,2,0,1:T(8,128)}, u32[]{:S(2)}, u32[]{:S(2)}) collective-permute-start(f32[8,2,8,256]{3,2,0,1:T(8,128)} %get-tuple-element.218), channel_id=1, source_target_pairs={{8,0},{16,8},{24,16},{32,24},{40,32},{48,40},{56,48},{64,56},{72,6... | collective-permute-start | bytes 393224 | tf_op jit(solution)/shard_map/while/body/eval_jaxpr/ppermute | solution.py:25
  73.1 2.8 multiply_bitcast_fusion.9
  87.9 6.8 %collective-permute-start.2 = (f32[8,2,16,256]{3,2,0,1:T(8,128)S(1)}, f32[8,2,16,256]{3,2,0,1:T(8,128)S(1)}, u32[]{:S(2)}, u32[]{:S(2)}) collective-permute-start(f32[8,2,16,256]{3,2,0,1:T(8,128)S(1)} %get-tuple-element.252), channel_id=1, source_target_pairs={{0,1},{1,2},{2,3},{3,4},{4,5},{5,6},{6,7},{8,9},{9,10},{10,11},{11... | collective-permute-start | bytes 786440 | tf_op jit(solution)/shard_map/while/body/eval_jaxpr/ppermute | solution.py:35
  96.6 1.9 collective-permute-start
  98.5 6.0 %collective-permute-start.1 = (f32[8,2,8,256]{3,2,0,1:T(8,128)}, f32[8,2,8,256]{3,2,0,1:T(8,128)}, u32[]{:S(2)}, u32[]{:S(2)}) collective-permute-start(f32[8,2,8,256]{3,2,0,1:T(8,128)} %get-tuple-element.218), channel_id=1, source_target_pairs={{8,0},{16,8},{24,16},{32,24},{40,32},{48,40},{56,48},{64,56},{72,6... | collective-permute-start | bytes 393224 | tf_op jit(solution)/shard_map/while/body/eval_jaxpr/ppermute | solution.py:25
  104.6 2.8 multiply_bitcast_fusion.9
  119.4 7.5 %collective-permute-start.2 = (f32[8,2,16,256]{3,2,0,1:T(8,128)S(1)}, f32[8,2,16,256]{3,2,0,1:T(8,128)S(1)}, u32[]{:S(2)}, u32[]{:S(2)}) collective-permute-start(f32[8,2,16,256]{3,2,0,1:T(8,128)S(1)} %get-tuple-element.252), channel_id=1, source_target_pairs={{0,1},{1,2},{2,3},{3,4},{4,5},{5,6},{6,7},{8,9},{9,10},{10,11},{11... | collective-permute-start | bytes 786440 | tf_op jit(solution)/shard_map/while/body/eval_jaxpr/ppermute | solution.py:35
  128.8 1.9 collective-permute-start
  130.7 6.0 %collective-permute-start.1 = (f32[8,2,8,256]{3,2,0,1:T(8,128)}, f32[8,2,8,256]{3,2,0,1:T(8,128)}, u32[]{:S(2)}, u32[]{:S(2)}) collective-permute-start(f32[8,2,8,256]{3,2,0,1:T(8,128)} %get-tuple-element.218), channel_id=1, source_target_pairs={{8,0},{16,8},{24,16},{32,24},{40,32},{48,40},{56,48},{64,56},{72,6... | collective-permute-start | bytes 393224 | tf_op jit(solution)/shard_map/while/body/eval_jaxpr/ppermute | solution.py:25
  136.8 2.8 multiply_bitcast_fusion.9
  151.5 7.6 %collective-permute-start.2 = (f32[8,2,16,256]{3,2,0,1:T(8,128)S(1)}, f32[8,2,16,256]{3,2,0,1:T(8,128)S(1)}, u32[]{:S(2)}, u32[]{:S(2)}) collective-permute-start(f32[8,2,16,256]{3,2,0,1:T(8,128)S(1)} %get-tuple-element.252), channel_id=1, source_target_pairs={{0,1},{1,2},{2,3},{3,4},{4,5},{5,6},{6,7},{8,9},{9,10},{10,11},{11... | collective-permute-start | bytes 786440 | tf_op jit(solution)/shard_map/while/body/eval_jaxpr/ppermute | solution.py:35
  161.0 1.9 collective-permute-start
  162.9 6.0 %collective-permute-start.1 = (f32[8,2,8,256]{3,2,0,1:T(8,128)}, f32[8,2,8,256]{3,2,0,1:T(8,128)}, u32[]{:S(2)}, u32[]{:S(2)}) collective-permute-start(f32[8,2,8,256]{3,2,0,1:T(8,128)} %get-tuple-element.218), channel_id=1, source_target_pairs={{8,0},{16,8},{24,16},{32,24},{40,32},{48,40},{56,48},{64,56},{72,6... | collective-permute-start | bytes 393224 | tf_op jit(solution)/shard_map/while/body/eval_jaxpr/ppermute | solution.py:25
  169.0 2.8 multiply_bitcast_fusion.9
  183.8 7.6 %collective-permute-start.2 = (f32[8,2,16,256]{3,2,0,1:T(8,128)S(1)}, f32[8,2,16,256]{3,2,0,1:T(8,128)S(1)}, u32[]{:S(2)}, u32[]{:S(2)}) collective-permute-start(f32[8,2,16,256]{3,2,0,1:T(8,128)S(1)} %get-tuple-element.252), channel_id=1, source_target_pairs={{0,1},{1,2},{2,3},{3,4},{4,5},{5,6},{6,7},{8,9},{9,10},{10,11},{11... | collective-permute-start | bytes 786440 | tf_op jit(solution)/shard_map/while/body/eval_jaxpr/ppermute | solution.py:35
  193.3 1.9 collective-permute-start
  195.2 6.0 %collective-permute-start.1 = (f32[8,2,8,256]{3,2,0,1:T(8,128)}, f32[8,2,8,256]{3,2,0,1:T(8,128)}, u32[]{:S(2)}, u32[]{:S(2)}) collective-permute-start(f32[8,2,8,256]{3,2,0,1:T(8,128)} %get-tuple-element.218), channel_id=1, source_target_pairs={{8,0},{16,8},{24,16},{32,24},{40,32},{48,40},{56,48},{64,56},{72,6... | collective-permute-start | bytes 393224 | tf_op jit(solution)/shard_map/while/body/eval_jaxpr/ppermute | solution.py:25
  201.3 2.8 multiply_bitcast_fusion.9
  216.0 7.6 %collective-permute-start.2 = (f32[8,2,16,256]{3,2,0,1:T(8,128)S(1)}, f32[8,2,16,256]{3,2,0,1:T(8,128)S(1)}, u32[]{:S(2)}, u32[]{:S(2)}) collective-permute-start(f32[8,2,16,256]{3,2,0,1:T(8,128)S(1)} %get-tuple-element.252), channel_id=1, source_target_pairs={{0,1},{1,2},{2,3},{3,4},{4,5},{5,6},{6,7},{8,9},{9,10},{10,11},{11... | collective-permute-start | bytes 786440 | tf_op jit(solution)/shard_map/while/body/eval_jaxpr/ppermute | solution.py:35
  225.5 1.9 collective-permute-start
  227.4 6.0 %collective-permute-start.1 = (f32[8,2,8,256]{3,2,0,1:T(8,128)}, f32[8,2,8,256]{3,2,0,1:T(8,128)}, u32[]{:S(2)}, u32[]{:S(2)}) collective-permute-start(f32[8,2,8,256]{3,2,0,1:T(8,128)} %get-tuple-element.218), channel_id=1, source_target_pairs={{8,0},{16,8},{24,16},{32,24},{40,32},{48,40},{56,48},{64,56},{72,6... | collective-permute-start | bytes 393224 | tf_op jit(solution)/shard_map/while/body/eval_jaxpr/ppermute | solution.py:25
  233.5 2.8 multiply_bitcast_fusion.9
  248.3 7.6 %collective-permute-start.2 = (f32[8,2,16,256]{3,2,0,1:T(8,128)S(1)}, f32[8,2,16,256]{3,2,0,1:T(8,128)S(1)}, u32[]{:S(2)}, u32[]{:S(2)}) collective-permute-start(f32[8,2,16,256]{3,2,0,1:T(8,128)S(1)} %get-tuple-element.252), channel_id=1, source_target_pairs={{0,1},{1,2},{2,3},{3,4},{4,5},{5,6},{6,7},{8,9},{9,10},{10,11},{11... | collective-permute-start | bytes 786440 | tf_op jit(solution)/shard_map/while/body/eval_jaxpr/ppermute | solution.py:35
  257.7 1.9 collective-permute-start
  259.7 6.0 %collective-permute-start.1 = (f32[8,2,8,256]{3,2,0,1:T(8,128)}, f32[8,2,8,256]{3,2,0,1:T(8,128)}, u32[]{:S(2)}, u32[]{:S(2)}) collective-permute-start(f32[8,2,8,256]{3,2,0,1:T(8,128)} %get-tuple-element.218), channel_id=1, source_target_pairs={{8,0},{16,8},{24,16},{32,24},{40,32},{48,40},{56,48},{64,56},{72,6... | collective-permute-start | bytes 393224 | tf_op jit(solution)/shard_map/while/body/eval_jaxpr/ppermute | solution.py:25
  265.8 2.8 multiply_bitcast_fusion.9
  280.5 7.8 %collective-permute-start.2 = (f32[8,2,16,256]{3,2,0,1:T(8,128)S(1)}, f32[8,2,16,256]{3,2,0,1:T(8,128)S(1)}, u32[]{:S(2)}, u32[]{:S(2)}) collective-permute-start(f32[8,2,16,256]{3,2,0,1:T(8,128)S(1)} %get-tuple-element.252), channel_id=1, source_target_pairs={{0,1},{1,2},{2,3},{3,4},{4,5},{5,6},{6,7},{8,9},{9,10},{10,11},{11... | collective-permute-start | bytes 786440 | tf_op jit(solution)/shard_map/while/body/eval_jaxpr/ppermute | solution.py:35
  289.5 2.8 fusion.33
  292.3 13.8 %copy.28 = f32[5,8,16,256]{0,2,1,3:T(8,128)} copy(f32[5,8,16,256]{3,0,2,1:T(8,128)S(1)} %fusion.33) | data formatting | bytes 1310720
  306.1 11.9 %reshape.263 = f32[256,640]{1,0:T(8,128)} reshape(f32[256,8,16,5]{3,2,1,0:T(8,128)} %bitcast.212) | data formatting | bytes 1310720
  318.1 43.6 %reduce-scatter.4.cloned.1.call-done = f32[64,640]{1,0:T(8,128)} async-done(((f32[256,640]{1,0:T(8,128)}), f32[64,640]{1,0:T(8,128)}) %reduce-scatter.4.cloned.1.call-update) | async-done | bytes 163856
  361.7 6.2 %reshape.264 = f32[64,8,16,5]{3,2,1,0:T(8,128)} reshape(f32[64,640]{1,0:T(8,128)} %reduce-scatter.4.cloned.1.call-done) | data formatting | bytes 327680
  368.0 3.8 copy.29
  373.0 1.7 reshape.265
  374.7 3.5 all-to-all-start
  378.2 9.9 %all-to-all-done = f32[4,1,40960]{2,1,0:T(1,128)S(1)} async-done(((f32[4,1,40960]{2,1,0:T(1,128)}), f32[4,1,40960]{2,1,0:T(1,128)S(1)}, u32[]{:S(2)}, u32[]{:S(2)}) %all-to-all-start) | async-done | bytes 655392 | tf_op jit(solution)/shard_map/all_to_all | solution.py:126
  388.6 2.5 reduce.4
  (640 shorter events, 121.0 us)
Async XLA Ops:
  7.2 354.6 %reduce-scatter.4.cloned.1.call-start = ((), (), s32[]{:S(2)}) async-start(), calls=%async_computation.2 | async-start | bytes 819200
  7.2 24.0 %copy-start.7 = (f32[5,8,16,256]{3,2,1,0:T(8,128)S(1)}, f32[5,8,16,256]{3,2,1,0:T(8,128)}, u32[]{:S(2)}) copy-start(f32[5,8,16,256]{3,2,1,0:T(8,128)} %param.11) | copy-start | bytes 1966084
  7.2 24.0 %copy-start.8 = (f32[8,16,256]{2,1,0:T(8,128)S(1)}, f32[8,16,256]{2,1,0:T(8,128)}, u32[]{:S(2)}) copy-start(f32[8,16,256]{2,1,0:T(8,128)} %param.10) | copy-start | bytes 393220
  7.2 24.0 %copy-start.12 = (f32[8,16,256]{2,1,0:T(8,128)S(1)}, f32[8,16,256]{2,1,0:T(8,128)}, u32[]{:S(2)}) copy-start(f32[8,16,256]{2,1,0:T(8,128)} %param.9) | copy-start | bytes 393220
  8.7 21.3 %collective-permute-start.3 = (f32[7,8,8,256]{3,2,1,0:T(8,128)S(1)}, f32[7,8,8,256]{3,2,1,0:T(8,128)S(1)}, u32[]{:S(2)}, u32[]{:S(2)}) collective-permute-start(f32[7,8,8,256]{3,2,1,0:T(8,128)S(1)} %get-tuple-element.112), channel_id=1, source_target_pairs={{0,8},{8,16},{16,24},{24,32},{32,40},{40,48},{48,56},{56,64},{64,7... | collective-permute-start | bytes 1376264 | tf_op jit(solution)/shard_map/ppermute | solution.py:23
  13.0 18.2 %collective-permute-start.4 = (f32[7,8,8,256]{3,2,1,0:T(8,128)S(1)}, f32[7,8,8,256]{3,2,1,0:T(8,128)}, u32[]{:S(2)}, u32[]{:S(2)}) collective-permute-start(f32[7,8,8,256]{3,2,1,0:T(8,128)S(1)} %get-tuple-element.113), channel_id=1, source_target_pairs={{8,0},{16,8},{24,16},{32,24},{40,32},{48,40},{56,48},{64,56},{72,6... | collective-permute-start | bytes 1376264 | tf_op jit(solution)/shard_map/ppermute | solution.py:25
  37.5 251.9 %copy-start.15 = (f32[8]{0:T(128)S(1)}, f32[8]{0:T(128)}, u32[]{:S(2)}) copy-start(f32[8]{0:T(128)} %param.13) | copy-start | bytes 100
  37.7 9.4 %copy-start.1 = (f32[8,2,16,256]{3,2,0,1:T(8,128)}, f32[8,2,16,256]{3,2,0,1:T(8,128)S(1)}, u32[]{:S(2)}) copy-start(f32[8,2,16,256]{3,2,0,1:T(8,128)S(1)} %get-tuple-element.263) | copy-start | bytes 786436 | tf_op jit(solution)/shard_map/while
  37.7 9.4 %copy-start.5 = (f32[8,32,256]{2,1,0:T(8,128)}, f32[8,32,256]{2,1,0:T(8,128)S(1)}, u32[]{:S(2)}) copy-start(f32[8,32,256]{2,1,0:T(8,128)S(1)} %get-tuple-element.273) | copy-start | bytes 786436 | tf_op jit(solution)/shard_map/while
  38.5 13.2 %collective-permute-start = (f32[8,2,8,256]{3,2,0,1:T(8,128)}, f32[8,2,8,256]{3,2,0,1:T(8,128)}, u32[]{:S(2)}, u32[]{:S(2)}) collective-permute-start(f32[8,2,8,256]{3,2,0,1:T(8,128)} %get-tuple-element.217), channel_id=1, source_target_pairs={{0,8},{8,16},{16,24},{24,32},{32,40},{40,48},{48,56},{56,64},{64,7... | collective-permute-start | bytes 393224 | tf_op jit(solution)/shard_map/while/body/eval_jaxpr/ppermute | solution.py:23
  40.5 13.2 %collective-permute-start.1 = (f32[8,2,8,256]{3,2,0,1:T(8,128)}, f32[8,2,8,256]{3,2,0,1:T(8,128)}, u32[]{:S(2)}, u32[]{:S(2)}) collective-permute-start(f32[8,2,8,256]{3,2,0,1:T(8,128)} %get-tuple-element.218), channel_id=1, source_target_pairs={{8,0},{16,8},{24,16},{32,24},{40,32},{48,40},{56,48},{64,56},{72,6... | collective-permute-start | bytes 393224 | tf_op jit(solution)/shard_map/while/body/eval_jaxpr/ppermute | solution.py:25
  61.9 2.4 collective-permute-start.2
  64.3 8.8 %copy-start.1 = (f32[8,2,16,256]{3,2,0,1:T(8,128)}, f32[8,2,16,256]{3,2,0,1:T(8,128)S(1)}, u32[]{:S(2)}) copy-start(f32[8,2,16,256]{3,2,0,1:T(8,128)S(1)} %get-tuple-element.263) | copy-start | bytes 786436 | tf_op jit(solution)/shard_map/while
  64.3 8.8 %copy-start.5 = (f32[8,32,256]{2,1,0:T(8,128)}, f32[8,32,256]{2,1,0:T(8,128)S(1)}, u32[]{:S(2)}) copy-start(f32[8,32,256]{2,1,0:T(8,128)S(1)} %get-tuple-element.273) | copy-start | bytes 786436 | tf_op jit(solution)/shard_map/while
  65.1 12.6 %collective-permute-start = (f32[8,2,8,256]{3,2,0,1:T(8,128)}, f32[8,2,8,256]{3,2,0,1:T(8,128)}, u32[]{:S(2)}, u32[]{:S(2)}) collective-permute-start(f32[8,2,8,256]{3,2,0,1:T(8,128)} %get-tuple-element.217), channel_id=1, source_target_pairs={{0,8},{8,16},{16,24},{24,32},{32,40},{40,48},{48,56},{56,64},{64,7... | collective-permute-start | bytes 393224 | tf_op jit(solution)/shard_map/while/body/eval_jaxpr/ppermute | solution.py:23
  67.0 12.6 %collective-permute-start.1 = (f32[8,2,8,256]{3,2,0,1:T(8,128)}, f32[8,2,8,256]{3,2,0,1:T(8,128)}, u32[]{:S(2)}, u32[]{:S(2)}) collective-permute-start(f32[8,2,8,256]{3,2,0,1:T(8,128)} %get-tuple-element.218), channel_id=1, source_target_pairs={{8,0},{16,8},{24,16},{32,24},{40,32},{48,40},{56,48},{64,56},{72,6... | collective-permute-start | bytes 393224 | tf_op jit(solution)/shard_map/while/body/eval_jaxpr/ppermute | solution.py:25
  87.9 8.0 %collective-permute-start.2 = (f32[8,2,16,256]{3,2,0,1:T(8,128)S(1)}, f32[8,2,16,256]{3,2,0,1:T(8,128)S(1)}, u32[]{:S(2)}, u32[]{:S(2)}) collective-permute-start(f32[8,2,16,256]{3,2,0,1:T(8,128)S(1)} %get-tuple-element.252), channel_id=1, source_target_pairs={{0,1},{1,2},{2,3},{3,4},{4,5},{5,6},{6,7},{8,9},{9,10},{10,11},{11... | collective-permute-start | bytes 786440 | tf_op jit(solution)/shard_map/while/body/eval_jaxpr/ppermute | solution.py:35
  95.8 8.8 %copy-start.1 = (f32[8,2,16,256]{3,2,0,1:T(8,128)}, f32[8,2,16,256]{3,2,0,1:T(8,128)S(1)}, u32[]{:S(2)}) copy-start(f32[8,2,16,256]{3,2,0,1:T(8,128)S(1)} %get-tuple-element.263) | copy-start | bytes 786436 | tf_op jit(solution)/shard_map/while
  95.8 8.8 %copy-start.5 = (f32[8,32,256]{2,1,0:T(8,128)}, f32[8,32,256]{2,1,0:T(8,128)S(1)}, u32[]{:S(2)}) copy-start(f32[8,32,256]{2,1,0:T(8,128)S(1)} %get-tuple-element.273) | copy-start | bytes 786436 | tf_op jit(solution)/shard_map/while
  96.6 12.6 %collective-permute-start = (f32[8,2,8,256]{3,2,0,1:T(8,128)}, f32[8,2,8,256]{3,2,0,1:T(8,128)}, u32[]{:S(2)}, u32[]{:S(2)}) collective-permute-start(f32[8,2,8,256]{3,2,0,1:T(8,128)} %get-tuple-element.217), channel_id=1, source_target_pairs={{0,8},{8,16},{16,24},{24,32},{32,40},{40,48},{48,56},{56,64},{64,7... | collective-permute-start | bytes 393224 | tf_op jit(solution)/shard_map/while/body/eval_jaxpr/ppermute | solution.py:23
  98.5 12.6 %collective-permute-start.1 = (f32[8,2,8,256]{3,2,0,1:T(8,128)}, f32[8,2,8,256]{3,2,0,1:T(8,128)}, u32[]{:S(2)}, u32[]{:S(2)}) collective-permute-start(f32[8,2,8,256]{3,2,0,1:T(8,128)} %get-tuple-element.218), channel_id=1, source_target_pairs={{8,0},{16,8},{24,16},{32,24},{40,32},{48,40},{56,48},{64,56},{72,6... | collective-permute-start | bytes 393224 | tf_op jit(solution)/shard_map/while/body/eval_jaxpr/ppermute | solution.py:25
  119.4 8.6 %collective-permute-start.2 = (f32[8,2,16,256]{3,2,0,1:T(8,128)S(1)}, f32[8,2,16,256]{3,2,0,1:T(8,128)S(1)}, u32[]{:S(2)}, u32[]{:S(2)}) collective-permute-start(f32[8,2,16,256]{3,2,0,1:T(8,128)S(1)} %get-tuple-element.252), channel_id=1, source_target_pairs={{0,1},{1,2},{2,3},{3,4},{4,5},{5,6},{6,7},{8,9},{9,10},{10,11},{11... | collective-permute-start | bytes 786440 | tf_op jit(solution)/shard_map/while/body/eval_jaxpr/ppermute | solution.py:35
  128.0 8.8 %copy-start.1 = (f32[8,2,16,256]{3,2,0,1:T(8,128)}, f32[8,2,16,256]{3,2,0,1:T(8,128)S(1)}, u32[]{:S(2)}) copy-start(f32[8,2,16,256]{3,2,0,1:T(8,128)S(1)} %get-tuple-element.263) | copy-start | bytes 786436 | tf_op jit(solution)/shard_map/while
  128.0 8.8 %copy-start.5 = (f32[8,32,256]{2,1,0:T(8,128)}, f32[8,32,256]{2,1,0:T(8,128)S(1)}, u32[]{:S(2)}) copy-start(f32[8,32,256]{2,1,0:T(8,128)S(1)} %get-tuple-element.273) | copy-start | bytes 786436 | tf_op jit(solution)/shard_map/while
  128.8 12.6 %collective-permute-start = (f32[8,2,8,256]{3,2,0,1:T(8,128)}, f32[8,2,8,256]{3,2,0,1:T(8,128)}, u32[]{:S(2)}, u32[]{:S(2)}) collective-permute-start(f32[8,2,8,256]{3,2,0,1:T(8,128)} %get-tuple-element.217), channel_id=1, source_target_pairs={{0,8},{8,16},{16,24},{24,32},{32,40},{40,48},{48,56},{56,64},{64,7... | collective-permute-start | bytes 393224 | tf_op jit(solution)/shard_map/while/body/eval_jaxpr/ppermute | solution.py:23
  130.7 12.6 %collective-permute-start.1 = (f32[8,2,8,256]{3,2,0,1:T(8,128)}, f32[8,2,8,256]{3,2,0,1:T(8,128)}, u32[]{:S(2)}, u32[]{:S(2)}) collective-permute-start(f32[8,2,8,256]{3,2,0,1:T(8,128)} %get-tuple-element.218), channel_id=1, source_target_pairs={{8,0},{16,8},{24,16},{32,24},{40,32},{48,40},{56,48},{64,56},{72,6... | collective-permute-start | bytes 393224 | tf_op jit(solution)/shard_map/while/body/eval_jaxpr/ppermute | solution.py:25
  151.5 8.7 %collective-permute-start.2 = (f32[8,2,16,256]{3,2,0,1:T(8,128)S(1)}, f32[8,2,16,256]{3,2,0,1:T(8,128)S(1)}, u32[]{:S(2)}, u32[]{:S(2)}) collective-permute-start(f32[8,2,16,256]{3,2,0,1:T(8,128)S(1)} %get-tuple-element.252), channel_id=1, source_target_pairs={{0,1},{1,2},{2,3},{3,4},{4,5},{5,6},{6,7},{8,9},{9,10},{10,11},{11... | collective-permute-start | bytes 786440 | tf_op jit(solution)/shard_map/while/body/eval_jaxpr/ppermute | solution.py:35
  160.2 8.8 %copy-start.1 = (f32[8,2,16,256]{3,2,0,1:T(8,128)}, f32[8,2,16,256]{3,2,0,1:T(8,128)S(1)}, u32[]{:S(2)}) copy-start(f32[8,2,16,256]{3,2,0,1:T(8,128)S(1)} %get-tuple-element.263) | copy-start | bytes 786436 | tf_op jit(solution)/shard_map/while
  160.2 8.8 %copy-start.5 = (f32[8,32,256]{2,1,0:T(8,128)}, f32[8,32,256]{2,1,0:T(8,128)S(1)}, u32[]{:S(2)}) copy-start(f32[8,32,256]{2,1,0:T(8,128)S(1)} %get-tuple-element.273) | copy-start | bytes 786436 | tf_op jit(solution)/shard_map/while
  161.0 12.6 %collective-permute-start = (f32[8,2,8,256]{3,2,0,1:T(8,128)}, f32[8,2,8,256]{3,2,0,1:T(8,128)}, u32[]{:S(2)}, u32[]{:S(2)}) collective-permute-start(f32[8,2,8,256]{3,2,0,1:T(8,128)} %get-tuple-element.217), channel_id=1, source_target_pairs={{0,8},{8,16},{16,24},{24,32},{32,40},{40,48},{48,56},{56,64},{64,7... | collective-permute-start | bytes 393224 | tf_op jit(solution)/shard_map/while/body/eval_jaxpr/ppermute | solution.py:23
  162.9 12.6 %collective-permute-start.1 = (f32[8,2,8,256]{3,2,0,1:T(8,128)}, f32[8,2,8,256]{3,2,0,1:T(8,128)}, u32[]{:S(2)}, u32[]{:S(2)}) collective-permute-start(f32[8,2,8,256]{3,2,0,1:T(8,128)} %get-tuple-element.218), channel_id=1, source_target_pairs={{8,0},{16,8},{24,16},{32,24},{40,32},{48,40},{56,48},{64,56},{72,6... | collective-permute-start | bytes 393224 | tf_op jit(solution)/shard_map/while/body/eval_jaxpr/ppermute | solution.py:25
  183.8 8.7 %collective-permute-start.2 = (f32[8,2,16,256]{3,2,0,1:T(8,128)S(1)}, f32[8,2,16,256]{3,2,0,1:T(8,128)S(1)}, u32[]{:S(2)}, u32[]{:S(2)}) collective-permute-start(f32[8,2,16,256]{3,2,0,1:T(8,128)S(1)} %get-tuple-element.252), channel_id=1, source_target_pairs={{0,1},{1,2},{2,3},{3,4},{4,5},{5,6},{6,7},{8,9},{9,10},{10,11},{11... | collective-permute-start | bytes 786440 | tf_op jit(solution)/shard_map/while/body/eval_jaxpr/ppermute | solution.py:35
  192.5 8.8 %copy-start.5 = (f32[8,32,256]{2,1,0:T(8,128)}, f32[8,32,256]{2,1,0:T(8,128)S(1)}, u32[]{:S(2)}) copy-start(f32[8,32,256]{2,1,0:T(8,128)S(1)} %get-tuple-element.273) | copy-start | bytes 786436 | tf_op jit(solution)/shard_map/while
  193.3 12.6 %collective-permute-start = (f32[8,2,8,256]{3,2,0,1:T(8,128)}, f32[8,2,8,256]{3,2,0,1:T(8,128)}, u32[]{:S(2)}, u32[]{:S(2)}) collective-permute-start(f32[8,2,8,256]{3,2,0,1:T(8,128)} %get-tuple-element.217), channel_id=1, source_target_pairs={{0,8},{8,16},{16,24},{24,32},{32,40},{40,48},{48,56},{56,64},{64,7... | collective-permute-start | bytes 393224 | tf_op jit(solution)/shard_map/while/body/eval_jaxpr/ppermute | solution.py:23
  195.2 12.6 %collective-permute-start.1 = (f32[8,2,8,256]{3,2,0,1:T(8,128)}, f32[8,2,8,256]{3,2,0,1:T(8,128)}, u32[]{:S(2)}, u32[]{:S(2)}) collective-permute-start(f32[8,2,8,256]{3,2,0,1:T(8,128)} %get-tuple-element.218), channel_id=1, source_target_pairs={{8,0},{16,8},{24,16},{32,24},{40,32},{48,40},{56,48},{64,56},{72,6... | collective-permute-start | bytes 393224 | tf_op jit(solution)/shard_map/while/body/eval_jaxpr/ppermute | solution.py:25
  216.0 8.7 %collective-permute-start.2 = (f32[8,2,16,256]{3,2,0,1:T(8,128)S(1)}, f32[8,2,16,256]{3,2,0,1:T(8,128)S(1)}, u32[]{:S(2)}, u32[]{:S(2)}) collective-permute-start(f32[8,2,16,256]{3,2,0,1:T(8,128)S(1)} %get-tuple-element.252), channel_id=1, source_target_pairs={{0,1},{1,2},{2,3},{3,4},{4,5},{5,6},{6,7},{8,9},{9,10},{10,11},{11... | collective-permute-start | bytes 786440 | tf_op jit(solution)/shard_map/while/body/eval_jaxpr/ppermute | solution.py:35
  224.7 8.8 %copy-start.1 = (f32[8,2,16,256]{3,2,0,1:T(8,128)}, f32[8,2,16,256]{3,2,0,1:T(8,128)S(1)}, u32[]{:S(2)}) copy-start(f32[8,2,16,256]{3,2,0,1:T(8,128)S(1)} %get-tuple-element.263) | copy-start | bytes 786436 | tf_op jit(solution)/shard_map/while
  224.7 8.8 %copy-start.5 = (f32[8,32,256]{2,1,0:T(8,128)}, f32[8,32,256]{2,1,0:T(8,128)S(1)}, u32[]{:S(2)}) copy-start(f32[8,32,256]{2,1,0:T(8,128)S(1)} %get-tuple-element.273) | copy-start | bytes 786436 | tf_op jit(solution)/shard_map/while
  225.5 12.6 %collective-permute-start = (f32[8,2,8,256]{3,2,0,1:T(8,128)}, f32[8,2,8,256]{3,2,0,1:T(8,128)}, u32[]{:S(2)}, u32[]{:S(2)}) collective-permute-start(f32[8,2,8,256]{3,2,0,1:T(8,128)} %get-tuple-element.217), channel_id=1, source_target_pairs={{0,8},{8,16},{16,24},{24,32},{32,40},{40,48},{48,56},{56,64},{64,7... | collective-permute-start | bytes 393224 | tf_op jit(solution)/shard_map/while/body/eval_jaxpr/ppermute | solution.py:23
  227.4 12.6 %collective-permute-start.1 = (f32[8,2,8,256]{3,2,0,1:T(8,128)}, f32[8,2,8,256]{3,2,0,1:T(8,128)}, u32[]{:S(2)}, u32[]{:S(2)}) collective-permute-start(f32[8,2,8,256]{3,2,0,1:T(8,128)} %get-tuple-element.218), channel_id=1, source_target_pairs={{8,0},{16,8},{24,16},{32,24},{40,32},{48,40},{56,48},{64,56},{72,6... | collective-permute-start | bytes 393224 | tf_op jit(solution)/shard_map/while/body/eval_jaxpr/ppermute | solution.py:25
  248.3 8.7 %collective-permute-start.2 = (f32[8,2,16,256]{3,2,0,1:T(8,128)S(1)}, f32[8,2,16,256]{3,2,0,1:T(8,128)S(1)}, u32[]{:S(2)}, u32[]{:S(2)}) collective-permute-start(f32[8,2,16,256]{3,2,0,1:T(8,128)S(1)} %get-tuple-element.252), channel_id=1, source_target_pairs={{0,1},{1,2},{2,3},{3,4},{4,5},{5,6},{6,7},{8,9},{9,10},{10,11},{11... | collective-permute-start | bytes 786440 | tf_op jit(solution)/shard_map/while/body/eval_jaxpr/ppermute | solution.py:35
  257.0 8.8 %copy-start.5 = (f32[8,32,256]{2,1,0:T(8,128)}, f32[8,32,256]{2,1,0:T(8,128)S(1)}, u32[]{:S(2)}) copy-start(f32[8,32,256]{2,1,0:T(8,128)S(1)} %get-tuple-element.273) | copy-start | bytes 786436 | tf_op jit(solution)/shard_map/while
  257.7 12.6 %collective-permute-start = (f32[8,2,8,256]{3,2,0,1:T(8,128)}, f32[8,2,8,256]{3,2,0,1:T(8,128)}, u32[]{:S(2)}, u32[]{:S(2)}) collective-permute-start(f32[8,2,8,256]{3,2,0,1:T(8,128)} %get-tuple-element.217), channel_id=1, source_target_pairs={{0,8},{8,16},{16,24},{24,32},{32,40},{40,48},{48,56},{56,64},{64,7... | collective-permute-start | bytes 393224 | tf_op jit(solution)/shard_map/while/body/eval_jaxpr/ppermute | solution.py:23
  259.7 12.6 %collective-permute-start.1 = (f32[8,2,8,256]{3,2,0,1:T(8,128)}, f32[8,2,8,256]{3,2,0,1:T(8,128)}, u32[]{:S(2)}, u32[]{:S(2)}) collective-permute-start(f32[8,2,8,256]{3,2,0,1:T(8,128)} %get-tuple-element.218), channel_id=1, source_target_pairs={{8,0},{16,8},{24,16},{32,24},{40,32},{48,40},{56,48},{64,56},{72,6... | collective-permute-start | bytes 393224 | tf_op jit(solution)/shard_map/while/body/eval_jaxpr/ppermute | solution.py:25
  280.4 9.1 %copy-start.6 = (f32[8,32,256]{2,1,0:T(8,128)S(1)}, f32[8,32,256]{2,1,0:T(8,128)}, u32[]{:S(2)}) copy-start(f32[8,32,256]{2,1,0:T(8,128)} %copy-done.5) | copy-start | bytes 786436 | tf_op jit(solution)/shard_map/while
  280.5 9.0 %collective-permute-start.2 = (f32[8,2,16,256]{3,2,0,1:T(8,128)S(1)}, f32[8,2,16,256]{3,2,0,1:T(8,128)S(1)}, u32[]{:S(2)}, u32[]{:S(2)}) collective-permute-start(f32[8,2,16,256]{3,2,0,1:T(8,128)S(1)} %get-tuple-element.252), channel_id=1, source_target_pairs={{0,1},{1,2},{2,3},{3,4},{4,5},{5,6},{6,7},{8,9},{9,10},{10,11},{11... | collective-permute-start | bytes 786440 | tf_op jit(solution)/shard_map/while/body/eval_jaxpr/ppermute | solution.py:35
  306.1 11.9 %copy-start.9 = (f32[8,16,256]{2,1,0:T(8,128)S(1)}, f32[8,16,256]{2,1,0:T(8,128)}, u32[]{:S(2)}) copy-start(f32[8,16,256]{2,1,0:T(8,128)} %param.10) | copy-start | bytes 393220
  374.7 13.4 %all-to-all-start = ((f32[4,1,40960]{2,1,0:T(1,128)}), f32[4,1,40960]{2,1,0:T(1,128)S(1)}, u32[]{:S(2)}, u32[]{:S(2)}) async-start(f32[4,1,40960]{2,1,0:T(1,128)} %reshape.265), calls=%async_computation | async-start | bytes 1310720 | tf_op jit(solution)/shard_map/all_to_all | solution.py:126
  (53 other events, 116.1 us)
Sparse Core Ops, SparseCore 0:
  318.1 43.5 reduce-scatter.3
